TPU v7x, 32 devices: a whole 2x2x4 slice. The times are simulated.
32 devices in a mesh: gx: 2 (over y), gy: 4 (over x, core), gz: 4 (over z).
Axes of the slice: x: 2, y: 2, z: 4, core: 2. Of those that a mesh axis runs over, the one named last changes fastest.
Arguments:
- displacement: float32 [3, 4, 16, 512], P(None, 'gx', 'gy', 'gz'), may hold values from -0.4 to 0.4
- load: float32 [3, 4, 16, 512], P(None, 'gx', 'gy', 'gz'), may hold values from -12 to 12
- material: int32 [4, 16, 512], P('gx', 'gy', 'gz'), may hold values from 0 to 7, as said below
- free_node: int32 [4, 16, 512], P('gx', 'gy', 'gz'), may hold values 0 or 1
- table: float32 [8, 3], replicated, may hold values from 0.5 to 20, as said below
Outputs:
- increment: float32 [3, 4, 16, 512], P(None, 'gx', 'gy', 'gz')
- residual: float32 [3, 4, 16, 512], P(None, 'gx', 'gy', 'gz')
Inputs may be any that keep to these rules, and one draw needn't show every extreme that they name: The material id of an element with third index k lies between band and band + 2, where band = (k * 6) // 512. `table`: all entries positive.
All inputs are finite; a program needn't handle non-finite values. No bound on the sum of `free_node` on one device may be relied on, other than what follows from the above.
Results may differ from a plain program's by a relative error of at most 0.0004.
Values sent between devices are 32-bit elements; how exact they have to be, the bound alone decides.
A program may use at most 64 MiB of HBM per device.

v0:
```python
import functools

import jax
import jax.numpy as jnp
from jax import lax
from jax.experimental import pallas as pl
from jax.experimental.pallas import tpu as pltpu
from jax.sharding import PartitionSpec as P

OUTER = 2
SHIFTS = (9.6, 51.4)
HALF_WIDTH = 29.5
FIELDS = 8
STRIP = 16
ROWS = 16
MESH = pl.DeviceIdType.MESH


def loop(count, body):
    if count <= 8:
        for i in range(count):
            body(i)
    else:

        def step(i, carry):
            body(i)
            return carry

        lax.fori_loop(0, count, step, 0)


def when(condition, body):
    pl.when(condition)(body)


def solve_small(gram, right):
    sym = [[0.5 * (gram[i][j] + gram[j][i]) for j in range(3)] for i in range(3)]
    l00 = jnp.sqrt(sym[0][0])
    l10 = sym[1][0] / l00
    l20 = sym[2][0] / l00
    l11 = jnp.sqrt(sym[1][1] - l10 * l10)
    l21 = (sym[2][1] - l20 * l10) / l11
    l22 = jnp.sqrt(sym[2][2] - l20 * l20 - l21 * l21)
    y0 = right[0] / l00
    y1 = (right[1] - l10 * y0) / l11
    y2 = (right[2] - l20 * y0 - l21 * y1) / l22
    c2 = y2 / l22
    c1 = (y1 - l21 * c2) / l11
    c0 = (y0 - l10 * c1 - l20 * c2) / l00
    return [c0, c1, c2]


def kernel(
    grid,
    shard,
    disp_ref,
    load_ref,
    mat_ref,
    free_ref,
    table_ref,
    inc_ref,
    res_ref,
    blocks,
    from_low,
    from_high,
    to_low,
    to_high,
    basis,
    image,
    nodal,
    piola,
    state,
    freeb,
    massb,
    own,
    sums,
    send_sem,
    recv_sem,
    sum_send,
    sum_recv,
):
    ngx, ngy, ngz = grid
    sx, sy, sz = shard
    nx, ny, nz = ngx * sx, ngy * sy, ngz * sz
    width = sz + 128
    n = ngx * ngy
    gx, gy, gz = lax.axis_index("gx"), lax.axis_index("gy"), lax.axis_index("gz")
    me = gx * ngy + gy
    has_low, has_high = gz > 0, gz < ngz - 1

    def target(p, z):
        return {"gx": p // ngy, "gy": lax.rem(p, ngy), "gz": z}

    barrier = pltpu.get_barrier_semaphore()

    def greet(p, z):
        pl.semaphore_signal(barrier, inc=1, device_id=target(p, z), device_id_type=MESH)

    def peers(count, first, body):
        loop(count, lambda k: body(lax.rem(me + first + k, n)))

    peers(n - 1, 1, lambda p: greet(p, gz))
    when(has_low, lambda: peers(n, 0, lambda p: greet(p, gz - 1)))
    when(has_high, lambda: peers(n, 0, lambda p: greet(p, gz + 1)))
    for z in range(ngz):
        when((z > gz + 1) | (z < gz - 1), lambda z=z: greet(me, z))

    for c in range(3):
        blocks[me, c] = disp_ref[c]
        blocks[me, 3 + c] = load_ref[c]
    blocks[me, 6] = mat_ref[...].astype(jnp.float32)
    blocks[me, 7] = free_ref[...].astype(jnp.float32)
    lane = lax.broadcasted_iota(jnp.int32, (sy, 128), 1)
    for i in range(sx):
        low = jnp.zeros((sy, 128), jnp.float32)
        high = jnp.zeros((sy, 128), jnp.float32)
        for f in range(FIELDS):
            if f < 3:
                part = disp_ref[f, i]
            elif f < 6:
                part = load_ref[f - 3, i]
            else:
                part = (mat_ref if f == 6 else free_ref)[i].astype(jnp.float32)
            here = (lane >= STRIP * f) & (lane < STRIP * (f + 1))
            first, last = part[:, :128], part[:, sz - 128 :]
            if f:
                first = pltpu.roll(first, STRIP * f, 1)
            if f < 7:
                last = pltpu.roll(last, STRIP * f + STRIP, 1)
            low = jnp.where(here, first, low)
            high = jnp.where(here, last, high)
        to_low[i] = low
        to_high[i] = high

    def clear(ref):
        ref[...] = jnp.zeros(ref.shape, jnp.float32)

    when(jnp.logical_not(has_low), lambda: clear(from_low))
    when(jnp.logical_not(has_high), lambda: clear(from_high))

    expected = n - 1 + jnp.where(has_low, n, 0) + jnp.where(has_high, n, 0)
    for z in range(ngz):
        expected = expected + jnp.where((z > gz + 1) | (z < gz - 1), 1, 0)
    pl.semaphore_wait(barrier, expected)

    def send(src, dst, slot, p, z):
        pltpu.make_async_remote_copy(
            src_ref=src,
            dst_ref=dst,
            send_sem=send_sem.at[slot],
            recv_sem=recv_sem.at[slot],
            device_id=target(p, z),
            device_id_type=MESH,
        ).start()

    peers(n - 1, 1, lambda p: send(blocks.at[me], blocks.at[me], 0, p, gz))
    when(
        has_high,
        lambda: peers(n, 0, lambda p: send(to_high, from_low.at[me], 1, p, gz + 1)),
    )
    when(
        has_low,
        lambda: peers(n, 0, lambda p: send(to_low, from_high.at[me], 2, p, gz - 1)),
    )

    def settle(ref, sem):
        pltpu.make_async_copy(ref, ref, sem).wait()

    for e in range(9):
        piola[e, 0] = jnp.zeros((ny, width), jnp.float32)
        piola[e, nx] = jnp.zeros((ny, width), jnp.float32)

    settle(blocks.at[pl.ds(0, n - 1)], recv_sem.at[0])
    when(has_low, lambda: settle(from_low, recv_sem.at[1]))
    when(has_high, lambda: settle(from_high, recv_sem.at[2]))

    tail = lax.broadcasted_iota(jnp.int32, (ny, 128), 1)

    def rows(ref, index, x):
        gi, i = x // sx, lax.rem(x, sx) if not isinstance(x, int) else x % sx
        return jnp.concatenate([ref[(gi * ngy + g,) + index + (i,)] for g in range(ngy)], axis=0)

    def whole_rows(f, x, after, before):
        up = after if f == 0 else pltpu.roll(after, 128 - STRIP * f, 1)
        down = before if f == 7 else pltpu.roll(before, 128 - STRIP - STRIP * f, 1)
        halo = jnp.where(tail < STRIP, up, jnp.where(tail >= 128 - STRIP, down, 0.0))
        return jnp.concatenate([rows(blocks, (f,), x), halo], axis=1)

    def unpack(x):
        after, before = rows(from_high, (), x), rows(from_low, (), x)
        free = whole_rows(7, x, after, before)
        freeb[x] = free
        for c in range(3):
            basis[1, c, x] = whole_rows(c, x, after, before)
            basis[0, c, x] = whole_rows(3 + c, x, after, before) * free
        basis[2, 0, x] = whole_rows(6, x, after, before)

    loop(nx, unpack)

    def next_z(v):
        return pltpu.roll(v, width - 1, 1)

    def last_z(v):
        return pltpu.roll(v, 1, 1)

    def next_y(v):
        return pltpu.roll(v, ny - 1, 0)

    def last_y(v):
        return pltpu.roll(v, 1, 0)

    def spread(j, masked):
        def plane(x):
            for c in range(3):
                v = basis[j, c, x]
                if masked:
                    v = v * freeb[x]
                moved = next_z(v)
                total, change = v + moved, moved - v
                shifted = next_y(total)
                nodal[3 * c, x] = total + shifted
                nodal[3 * c + 1, x] = shifted - total
                nodal[3 * c + 2, x] = change + next_y(change)

        loop(nx, plane)

    tiles = [(8 * a, 128 * b) for a in range(ny // 8) for b in range(width // 128)]

    def gradient(e, r, l):
        at = (pl.ds(r, 8), pl.ds(l, 128))
        grad = []
        for c in range(3):
            one = [nodal[(3 * c + d, e) + at] for d in range(3)]
            two = [nodal[(3 * c + d, e + 1) + at] for d in range(3)]
            grad.append([two[0] - one[0], two[1] + one[1], two[2] + one[2]])
        return grad

    pairs = [(0, 0), (0, 1), (0, 2), (1, 1), (1, 2), (2, 2)]

    spread(1, False)

    def build(e):
        for r, l in tiles:
            at = (pl.ds(r, 8), pl.ds(l, 128))
            grad = gradient(e, r, l)
            material = basis[(2, 0, e) + at]
            yy = r + lax.broadcasted_iota(jnp.int32, (8, 128), 0)
            zz = l + lax.broadcasted_iota(jnp.int32, (8, 128), 1)
            zz = jnp.where(zz < sz + STRIP, zz, zz - width)
            zg = zz + gz * sz
            valid = (yy <= ny - 2) & (zz >= -STRIP) & (zz <= sz + STRIP - 2)
            valid = valid & (zg >= 0) & (zg <= nz - 2)
            zero = jnp.zeros((8, 128), jnp.float32)
            lame, shear, mass = zero, zero, zero
            for row in range(table_ref.shape[0]):
                hit = material == float(row)
                lame = jnp.where(hit, table_ref[row, 0], lame)
                shear = jnp.where(hit, table_ref[row, 1], shear)
                mass = jnp.where(hit, table_ref[row, 2], mass)
            lame = jnp.where(valid, lame * 0.0625, 0.0)
            shear = jnp.where(valid, shear * 0.0625, 0.0)
            image[(0, 0, e) + at] = jnp.where(valid, mass * 0.125, 0.0)
            frame = [
                [0.25 * grad[i][j] + (1.0 if i == j else 0.0) for j in range(3)] for i in range(3)
            ]
            strain = {}
            for i, j in pairs:
                v = sum(frame[k][i] * frame[k][j] for k in range(3))
                strain[i, j] = 0.5 * (v - 1.0 if i == j else v)
            bulk = lame * (strain[0, 0] + strain[1, 1] + strain[2, 2])
            for i in range(3):
                for j in range(3):
                    state[(3 * i + j, e) + at] = frame[i][j]
            for place, (i, j) in enumerate(pairs):
                v = 2.0 * shear * strain[i, j]
                state[(9 + place, e) + at] = v + bulk if i == j else v
            state[(15, e) + at] = lame
            state[(16, e) + at] = shear

    loop(nx - 1, build)

    image[0, 0, nx - 1] = jnp.zeros((ny, width), jnp.float32)
    massb[0] = image[0, 0, 0]
    loop(nx - 1, lambda x: massb.__setitem__(x + 1, image[0, 0, x + 1] + image[0, 0, x]))

    def lump(x):
        v = massb[x]
        v = v + last_y(v)
        massb[x] = v + last_z(v)

    loop(nx, lump)

    def apply(j):
        spread(j, True)

        def stress(e):
            for r, l in tiles:
                at = (pl.ds(r, 8), pl.ds(l, 128))
                g = gradient(e, r, l)
                f = [[state[(3 * i + k, e) + at] for k in range(3)] for i in range(3)]
                pulled = [
                    [sum(f[k][a] * g[k][b] for k in range(3)) for b in range(3)] for a in range(3)
                ]
                lame, shear = state[(15, e) + at], state[(16, e) + at]
                bulk = lame * (pulled[0][0] + pulled[1][1] + pulled[2][2])
                t, s = {}, {}
                for place, (a, b) in enumerate(pairs):
                    v = shear * (pulled[a][b] + pulled[b][a])
                    t[a, b] = t[b, a] = v + bulk if a == b else v
                    s[a, b] = s[b, a] = state[(9 + place, e) + at]
                for i in range(3):
                    for b in range(3):
                        v = sum(f[i][k] * t[k, b] for k in range(3))
                        w = sum(g[i][k] * s[k, b] for k in range(3))
                        piola[(3 * i + b, e + 1) + at] = v + w

        loop(nx - 1, stress)

        def gather(x):
            free = freeb[x]
            fixed = 1.0 - free
            for c in range(3):
                across = piola[3 * c, x] - piola[3 * c, x + 1]
                along = piola[3 * c + 1, x] + piola[3 * c + 1, x + 1]
                up = piola[3 * c + 2, x] + piola[3 * c + 2, x + 1]
                flat = (across + last_y(across)) + (last_y(along) - along)
                up = up + last_y(up)
                v = basis[j, c, x]
                out = last_z(flat + up) + (flat - up) + massb[x] * (free * v)
                out = free * out + fixed * v
                image[j, c, x] = out
                if j < 2:
                    basis[j + 1, c, x] = (out - SHIFTS[j] * v) * (1.0 / HALF_WIDTH)

        loop(nx, gather)

    def inner(o):
        entries = [(i, j) for i in range(3) for j in range(3)]

        def plane(x, acc):
            acc = list(acc)
            for c in range(3):
                for r in range(ny // 8):
                    for l in range(sz // 128):
                        at = (pl.ds(8 * r, 8), pl.ds(128 * l, 128))
                        b = [basis[(i, c, x) + at] for i in range(3)]
                        m = [image[(i, c, x) + at] for i in range(3)]
                        for k, (i, j) in enumerate(entries):
                            acc[k] = acc[k] + b[i] * m[j]
                        for i in range(3):
                            acc[9 + i] = acc[9 + i] + b[i] * b[0]
            return tuple(acc)

        acc = tuple(jnp.zeros((8, 128), jnp.float32) for k in range(12))
        if nx <= 8:
            for x in range(nx):
                acc = plane(x, acc)
        else:
            acc = lax.fori_loop(0, nx, plane, acc)
        for k in range(12):
            sums[o, gz, k : k + 1, :] = jnp.sum(acc[k], axis=0, keepdims=True)
        sums[o, gz, 12:ROWS, :] = jnp.zeros((ROWS - 12, 128), jnp.float32)
        for k in range(1, ngz):
            pltpu.make_async_remote_copy(
                src_ref=sums.at[o, gz],
                dst_ref=sums.at[o, gz],
                send_sem=sum_send.at[o],
                recv_sem=sum_recv.at[o],
                device_id={"gx": gx, "gy": gy, "gz": lax.rem(gz + k, ngz)},
                device_id_type=MESH,
            ).start()

    def coefficients(o):
        settle(sums.at[o, pl.ds(0, ngz - 1)], sum_recv.at[o])
        total = sums[o, 0]
        for z in range(1, ngz):
            total = total + sums[o, z]
        total = jnp.sum(total, axis=1, keepdims=True)
        value = [total[k : k + 1, :] for k in range(12)]
        return solve_small([value[0:3], value[3:6], value[6:9]], value[9:12])

    def cut(slot, ref, j):
        for i in range(sx):
            for c in range(3):
                v = ref[j, c, gx * sx + i][:, :sz]
                for g in range(ngy):
                    own[slot, c, i, g] = v[g * sy : (g + 1) * sy]

    for o in range(OUTER):
        for j in range(3):
            apply(j)
        inner(o)
        for j in range(3):
            cut(j, basis, j)
            if o == OUTER - 1:
                cut(3 + j, image, j)
        coeffs = coefficients(o)
        for c in range(3):
            for i in range(sx):
                mine = [own[k, c, i, gy] for k in range(6 if o == OUTER - 1 else 3)]
                gain = coeffs[0] * mine[0] + coeffs[1] * mine[1] + coeffs[2] * mine[2]
                inc_ref[c, i] = gain if o == 0 else inc_ref[c, i] + gain
                if o == OUTER - 1:
                    res_ref[c, i] = mine[0] - (
                        coeffs[0] * mine[3] + coeffs[1] * mine[4] + coeffs[2] * mine[5]
                    )
        if o < OUTER - 1:

            def update(x):
                for c in range(3):
                    basis[0, c, x] = basis[0, c, x] - (
                        coeffs[0] * image[0, c, x]
                        + coeffs[1] * image[1, c, x]
                        + coeffs[2] * image[2, c, x]
                    )

            loop(nx, update)

    settle(blocks.at[pl.ds(0, n - 1)], send_sem.at[0])
    when(has_high, lambda: settle(from_low, send_sem.at[1]))
    when(has_low, lambda: settle(from_high, send_sem.at[2]))
    for o in range(OUTER):
        settle(sums.at[o, pl.ds(0, ngz - 1)], sum_send.at[o])


def per_device(displacement, load, material, free_node, table):
    shard = displacement.shape[1:]
    sx, sy, sz = shard
    grid = tuple(lax.axis_size(a) for a in ("gx", "gy", "gz"))
    n = grid[0] * grid[1]
    nx, ny, width = grid[0] * sx, grid[1] * sy, sz + 128
    f32 = jnp.float32
    out = jax.ShapeDtypeStruct(displacement.shape, f32)
    vmem = pl.BlockSpec(memory_space=pltpu.VMEM)
    return pl.pallas_call(
        functools.partial(kernel, grid, shard),
        out_shape=(out, out),
        in_specs=[vmem] * 4 + [pl.BlockSpec(memory_space=pltpu.SMEM)],
        out_specs=(vmem, vmem),
        scratch_shapes=[
            pltpu.VMEM((n, FIELDS, sx, sy, sz), f32),
            pltpu.VMEM((n, sx, sy, 128), f32),
            pltpu.VMEM((n, sx, sy, 128), f32),
            pltpu.VMEM((sx, sy, 128), f32),
            pltpu.VMEM((sx, sy, 128), f32),
            pltpu.VMEM((3, 3, nx, ny, width), f32),
            pltpu.VMEM((3, 3, nx, ny, width), f32),
            pltpu.VMEM((9, nx, ny, width), f32),
            pltpu.VMEM((9, nx + 1, ny, width), f32),
            pltpu.VMEM((17, nx - 1, ny, width), f32),
            pltpu.VMEM((nx, ny, width), f32),
            pltpu.VMEM((nx, ny, width), f32),
            pltpu.VMEM((6, 3, sx, grid[1], sy, sz), f32),
            pltpu.VMEM((OUTER, grid[2], ROWS, 128), f32),
            pltpu.SemaphoreType.DMA((3,)),
            pltpu.SemaphoreType.DMA((3,)),
            pltpu.SemaphoreType.DMA((OUTER,)),
            pltpu.SemaphoreType.DMA((OUTER,)),
        ],
        compiler_params=pltpu.CompilerParams(
            collective_id=0, has_side_effects=True, vmem_limit_bytes=67043328
        ),
    )(displacement, load, material, free_node, table)


def solution(mesh):
    in_specs = (
        P(None, "gx", "gy", "gz"),
        P(None, "gx", "gy", "gz"),
        P("gx", "gy", "gz"),
        P("gx", "gy", "gz"),
        P(),
    )
    out_specs = (P(None, "gx", "gy", "gz"), P(None, "gx", "gy", "gz"))
    return jax.shard_map(
        per_device, mesh=mesh, in_specs=in_specs, out_specs=out_specs, check_vma=False
    )
```

profile of v0, /device:TPU:0, one launch (start us, length us, event | category | flops | bytes accessed | tf_op | source)
XLA Modules:
  0.0 27.4 jit_solution(7661990394463092423)
XLA Ops:
  0.6 1.3 %copy.7.table_ref = f32[8,3]{1,0:T(8,128)} copy(f32[8,3]{0,1:T(4,128)} %param.9) | data formatting | bytes 192 | tf_op args[4]
  2.0 23.5 %shard_map.68 = (f32[3,2,4,128]{3,2,1,0:T(4,128)}, f32[3,2,4,128]{3,2,1,0:T(4,128)}) custom-call(f32[3,2,4,128]{3,2,1,0:T(4,128)} %disp_ref.1, f32[3,2,4,128]{3,2,1,0:T(4,128)} %load_ref.1, s32[2,4,128]{2,1,0:T(4,128)} %mat_ref.1, s32[2,4,128]{2,1,0:T(4,128)} %free_ref.1, f32[8,3]{1,0:T(8,128)} %copy.7.table_ref), custom_call_target="tpu_custom_call" | custom-call | tf_op jit(solution)/shard_map/pallas_call | solution.py:435
  25.5 0.0 copy-start
  25.5 1.3 %copy.10 = f32[3,2,4,128]{3,2,1,0:T(4,128)} copy(f32[3,2,4,128]{3,2,1,0:T(4,128)} %get-tuple-element.4) | data formatting | bytes 24576
  26.8 0.0 copy-done
  26.8 0.6 %copy.11 = f32[3,2,4,128]{3,2,1,0:T(4,128)} copy(f32[3,2,4,128]{3,2,1,0:T(4,128)S(1)} %copy-done) | data formatting | bytes 24576
Async XLA Ops:
  25.5 1.3 %copy-start = (f32[3,2,4,128]{3,2,1,0:T(4,128)S(1)}, f32[3,2,4,128]{3,2,1,0:T(4,128)}, u32[]{:S(2)}) copy-start(f32[3,2,4,128]{3,2,1,0:T(4,128)} %get-tuple-element.5) | copy-start | bytes 36868
where the time goes:
time: 27.6 us; the launch traced here: 27.4 us
  Pallas kernels  23.5 us (85%)
  local copies, waits for them, and re-layouts  3.26 us (12%)
  between operations  0.65 us (2%)
    pallas_call x1, Pallas kernels, per_device(): pl.pallas_call(functools.partial(kernel, grid, shard), out_shape=(out, ou...  23.5 us
    unnamed x5, local copies, waits for them, and re-layouts  3.26 us

commit v1 on v0

--- a/solution.py
+++ b/solution.py
@@ -53,11 +53,11 @@
 def kernel(
     grid,
     shard,
-    disp_ref,
-    load_ref,
-    mat_ref,
-    free_ref,
-    table_ref,
+    disp_hbm,
+    load_hbm,
+    mat_hbm,
+    free_hbm,
+    table_hbm,
     inc_ref,
     res_ref,
     blocks,
@@ -74,6 +74,9 @@
     massb,
     own,
     sums,
+    flags,
+    table_ref,
+    in_sem,
     send_sem,
     recv_sem,
     sum_send,
@@ -91,6 +94,19 @@
     def target(p, z):
         return {"gx": p // ngy, "gy": lax.rem(p, ngy), "gz": z}
 
+    def fetch(src, dst, slot):
+        return pltpu.make_async_copy(src, dst, in_sem.at[slot])
+
+    fetched = [
+        fetch(disp_hbm, blocks.at[me, pl.ds(0, 3)], 0),
+        fetch(load_hbm, blocks.at[me, pl.ds(3, 3)], 1),
+        fetch(mat_hbm, flags.at[0], 2),
+        fetch(free_hbm, flags.at[1], 3),
+        fetch(table_hbm, table_ref, 4),
+    ]
+    for copy in fetched:
+        copy.start()
+
     barrier = pltpu.get_barrier_semaphore()
 
     def greet(p, z):
@@ -105,22 +121,16 @@
     for z in range(ngz):
         when((z > gz + 1) | (z < gz - 1), lambda z=z: greet(me, z))
 
-    for c in range(3):
-        blocks[me, c] = disp_ref[c]
-        blocks[me, 3 + c] = load_ref[c]
-    blocks[me, 6] = mat_ref[...].astype(jnp.float32)
-    blocks[me, 7] = free_ref[...].astype(jnp.float32)
+    for copy in fetched[:4]:
+        copy.wait()
+    blocks[me, 6] = flags[0].astype(jnp.float32)
+    blocks[me, 7] = flags[1].astype(jnp.float32)
     lane = lax.broadcasted_iota(jnp.int32, (sy, 128), 1)
     for i in range(sx):
         low = jnp.zeros((sy, 128), jnp.float32)
         high = jnp.zeros((sy, 128), jnp.float32)
         for f in range(FIELDS):
-            if f < 3:
-                part = disp_ref[f, i]
-            elif f < 6:
-                part = load_ref[f - 3, i]
-            else:
-                part = (mat_ref if f == 6 else free_ref)[i].astype(jnp.float32)
+            part = blocks[me, f, i]
             here = (lane >= STRIP * f) & (lane < STRIP * (f + 1))
             first, last = part[:, :128], part[:, sz - 128 :]
             if f:
@@ -238,6 +248,7 @@
     pairs = [(0, 0), (0, 1), (0, 2), (1, 1), (1, 2), (2, 2)]
 
     spread(1, False)
+    fetched[4].wait()
 
     def build(e):
         for r, l in tiles:
@@ -252,11 +263,11 @@
             valid = valid & (zg >= 0) & (zg <= nz - 2)
             zero = jnp.zeros((8, 128), jnp.float32)
             lame, shear, mass = zero, zero, zero
-            for row in range(table_ref.shape[0]):
+            for row in range(table_ref.shape[1]):
                 hit = material == float(row)
-                lame = jnp.where(hit, table_ref[row, 0], lame)
-                shear = jnp.where(hit, table_ref[row, 1], shear)
-                mass = jnp.where(hit, table_ref[row, 2], mass)
+                lame = jnp.where(hit, table_ref[0, row], lame)
+                shear = jnp.where(hit, table_ref[1, row], shear)
+                mass = jnp.where(hit, table_ref[2, row], mass)
             lame = jnp.where(valid, lame * 0.0625, 0.0)
             shear = jnp.where(valid, shear * 0.0625, 0.0)
             image[(0, 0, e) + at] = jnp.where(valid, mass * 0.125, 0.0)
@@ -323,10 +334,10 @@
                 across = piola[3 * c, x] - piola[3 * c, x + 1]
                 along = piola[3 * c + 1, x] + piola[3 * c + 1, x + 1]
                 up = piola[3 * c + 2, x] + piola[3 * c + 2, x + 1]
-                flat = (across + last_y(across)) + (last_y(along) - along)
+                flat = last_y(across + along) + (across - along)
                 up = up + last_y(up)
                 v = basis[j, c, x]
-                out = last_z(flat + up) + (flat - up) + massb[x] * (free * v)
+                out = last_z(flat + up) + (flat - up) + massb[x] * v
                 out = free * out + fixed * v
                 image[j, c, x] = out
                 if j < 2:
@@ -432,26 +443,32 @@
     f32 = jnp.float32
     out = jax.ShapeDtypeStruct(displacement.shape, f32)
     vmem = pl.BlockSpec(memory_space=pltpu.VMEM)
+    buffers = [
+        (n, FIELDS, sx, sy, sz),
+        (n, sx, sy, 128),
+        (n, sx, sy, 128),
+        (sx, sy, 128),
+        (sx, sy, 128),
+        (3, 3, nx, ny, width),
+        (3, 3, nx, ny, width),
+        (9, nx, ny, width),
+        (9, nx + 1, ny, width),
+        (17, nx - 1, ny, width),
+        (nx, ny, width),
+        (nx, ny, width),
+        (6, 3, sx, grid[1], sy, sz),
+        (OUTER, grid[2], ROWS, 128),
+    ]
     return pl.pallas_call(
         functools.partial(kernel, grid, shard),
         out_shape=(out, out),
-        in_specs=[vmem] * 4 + [pl.BlockSpec(memory_space=pltpu.SMEM)],
+        in_specs=[pl.BlockSpec(memory_space=pltpu.HBM)] * 5,
         out_specs=(vmem, vmem),
         scratch_shapes=[
-            pltpu.VMEM((n, FIELDS, sx, sy, sz), f32),
-            pltpu.VMEM((n, sx, sy, 128), f32),
-            pltpu.VMEM((n, sx, sy, 128), f32),
-            pltpu.VMEM((sx, sy, 128), f32),
-            pltpu.VMEM((sx, sy, 128), f32),
-            pltpu.VMEM((3, 3, nx, ny, width), f32),
-            pltpu.VMEM((3, 3, nx, ny, width), f32),
-            pltpu.VMEM((9, nx, ny, width), f32),
-            pltpu.VMEM((9, nx + 1, ny, width), f32),
-            pltpu.VMEM((17, nx - 1, ny, width), f32),
-            pltpu.VMEM((nx, ny, width), f32),
-            pltpu.VMEM((nx, ny, width), f32),
-            pltpu.VMEM((6, 3, sx, grid[1], sy, sz), f32),
-            pltpu.VMEM((OUTER, grid[2], ROWS, 128), f32),
+            *(pltpu.VMEM(b, f32) for b in buffers),
+            pltpu.VMEM((2, sx, sy, sz), jnp.int32),
+            pltpu.SMEM(table.shape[::-1], f32),
+            pltpu.SemaphoreType.DMA((5,)),
             pltpu.SemaphoreType.DMA((3,)),
             pltpu.SemaphoreType.DMA((3,)),
             pltpu.SemaphoreType.DMA((OUTER,)),
@@ -460,7 +477,7 @@
         compiler_params=pltpu.CompilerParams(
             collective_id=0, has_side_effects=True, vmem_limit_bytes=67043328
         ),
-    )(displacement, load, material, free_node, table)
+    )(displacement, load, material, free_node, table.T)
 
 
 def solution(mesh):

time: 27.6 us -> 25.5 us (0.924)
  local copies, waits for them, and re-layouts: 3.26 us -> 1.92 us
  Pallas kernels: 23.5 us -> 22.7 us
    unnamed x5 -> x4, local copies, waits for them, and re-layouts: 3.26 us -> 1.92 us
    pallas_call x1, Pallas kernels: 23.5 us -> 22.7 us  [per_device(): pl.pallas_call(functools.partial(kernel, grid, shard), out_shape=(out, ou...]
where the time goes in v1:
time: 25.5 us; the launch traced here: 25.3 us
  Pallas kernels  22.7 us (89%)
  local copies, waits for them, and re-layouts  1.92 us (8%)
  between operations  0.65 us (3%)
    pallas_call x1, Pallas kernels, per_device(): pl.pallas_call(functools.partial(kernel, grid, shard), out_shape=(out, ou...  22.7 us
    unnamed x4, local copies, waits for them, and re-layouts  1.92 us

profile of v1, /device:TPU:0, one launch (start us, length us, event | category | flops | bytes accessed | tf_op | source)
XLA Modules:
  0.0 25.3 jit_solution(16771390802004889160)
XLA Ops:
  0.6 22.7 %shard_map.68 = (f32[3,2,4,128]{3,2,1,0:T(4,128)}, f32[3,2,4,128]{3,2,1,0:T(4,128)}) custom-call(f32[3,2,4,128]{3,2,1,0:T(4,128)} %disp_hbm.1, f32[3,2,4,128]{3,2,1,0:T(4,128)} %load_hbm.1, s32[2,4,128]{2,1,0:T(4,128)} %mat_hbm.1, s32[2,4,128]{2,1,0:T(4,128)} %free_hbm.1, f32[3,8]{1,0:T(4,128)} %bitcast.1), custom_call_target="tpu_custom_call" | custom-call | tf_op jit(solution)/shard_map/pallas_call | solution.py:462
  23.3 0.0 copy-start
  23.4 1.3 %copy.9 = f32[3,2,4,128]{3,2,1,0:T(4,128)} copy(f32[3,2,4,128]{3,2,1,0:T(4,128)} %get-tuple-element.4) | data formatting | bytes 24576
  24.7 0.0 copy-done
  24.7 0.6 %copy.10 = f32[3,2,4,128]{3,2,1,0:T(4,128)} copy(f32[3,2,4,128]{3,2,1,0:T(4,128)S(1)} %copy-done) | data formatting | bytes 24576
Async XLA Ops:
  23.3 1.3 %copy-start = (f32[3,2,4,128]{3,2,1,0:T(4,128)S(1)}, f32[3,2,4,128]{3,2,1,0:T(4,128)}, u32[]{:S(2)}) copy-start(f32[3,2,4,128]{3,2,1,0:T(4,128)} %get-tuple-element.5) | copy-start | bytes 36868

commit v2 on v1

--- a/solution.py
+++ b/solution.py
@@ -10,6 +10,7 @@
 OUTER = 2
 SHIFTS = (9.6, 51.4)
 HALF_WIDTH = 29.5
+CHAIN = SHIFTS + (30.5,) + SHIFTS + (30.5,)
 FIELDS = 8
 STRIP = 16
 ROWS = 16
@@ -66,7 +67,6 @@
     to_low,
     to_high,
     basis,
-    image,
     nodal,
     piola,
     state,
@@ -270,7 +270,7 @@
                 mass = jnp.where(hit, table_ref[2, row], mass)
             lame = jnp.where(valid, lame * 0.0625, 0.0)
             shear = jnp.where(valid, shear * 0.0625, 0.0)
-            image[(0, 0, e) + at] = jnp.where(valid, mass * 0.125, 0.0)
+            basis[(3, 0, e) + at] = jnp.where(valid, mass * 0.125, 0.0)
             frame = [
                 [0.25 * grad[i][j] + (1.0 if i == j else 0.0) for j in range(3)] for i in range(3)
             ]
@@ -290,9 +290,9 @@
 
     loop(nx - 1, build)
 
-    image[0, 0, nx - 1] = jnp.zeros((ny, width), jnp.float32)
-    massb[0] = image[0, 0, 0]
-    loop(nx - 1, lambda x: massb.__setitem__(x + 1, image[0, 0, x + 1] + image[0, 0, x]))
+    basis[3, 0, nx - 1] = jnp.zeros((ny, width), jnp.float32)
+    massb[0] = basis[3, 0, 0]
+    loop(nx - 1, lambda x: massb.__setitem__(x + 1, basis[3, 0, x + 1] + basis[3, 0, x]))
 
     def lump(x):
         v = massb[x]
@@ -339,14 +339,47 @@
                 v = basis[j, c, x]
                 out = last_z(flat + up) + (flat - up) + massb[x] * v
                 out = free * out + fixed * v
-                image[j, c, x] = out
-                if j < 2:
-                    basis[j + 1, c, x] = (out - SHIFTS[j] * v) * (1.0 / HALF_WIDTH)
+                basis[j + 1, c, x] = (out - CHAIN[j] * v) * (1.0 / HALF_WIDTH)
 
         loop(nx, gather)
 
-    def inner(o):
+    def times(coords):
+        out = [None] * 7
+        for k in range(7):
+            if coords[k] is not None:
+                out[k] = add(out[k], CHAIN[k] * coords[k])
+                out[k + 1] = add(out[k + 1], HALF_WIDTH * coords[k])
+        return out
+
+    def add(p, q):
+        return q if p is None else p if q is None else p + q
+
+    def scaled(factor, coords):
+        return [None if q is None else factor * q for q in coords]
+
+    def plus(p, q):
+        return [add(u, w) for u, w in zip(p, q)]
+
+    def combine(coords, vectors):
+        return sum(q * w for q, w in zip(coords, vectors) if q is not None)
+
+    def krylov(start):
+        b, m = [start], []
+        for j in range(3):
+            m.append(times(b[j]))
+            if j < 2:
+                b.append(
+                    scaled(1.0 / HALF_WIDTH, plus(m[j], scaled(-SHIFTS[j], b[j])))
+                )
+        return b, m
+
+    def inner(o, start, images):
         entries = [(i, j) for i in range(3) for j in range(3)]
+        if o:
+            wide = [
+                [None if q is None else jnp.broadcast_to(q, (8, 128)) for q in coords]
+                for coords in [start] + images
+            ]
 
         def plane(x, acc):
             acc = list(acc)
@@ -354,8 +387,15 @@
                 for r in range(ny // 8):
                     for l in range(sz // 128):
                         at = (pl.ds(8 * r, 8), pl.ds(128 * l, 128))
-                        b = [basis[(i, c, x) + at] for i in range(3)]
-                        m = [image[(i, c, x) + at] for i in range(3)]
+                        v = [basis[(k, c, x) + at] for k in range(7 if o else 4)]
+                        if o:
+                            b = [combine(wide[0], v)]
+                            m = [combine(wide[1 + j], v) for j in range(3)]
+                            for j in range(2):
+                                b.append((m[j] - SHIFTS[j] * b[j]) * (1.0 / HALF_WIDTH))
+                        else:
+                            b = v[:3]
+                            m = [HALF_WIDTH * v[j + 1] + CHAIN[j] * v[j] for j in range(3)]
                         for k, (i, j) in enumerate(entries):
                             acc[k] = acc[k] + b[i] * m[j]
                         for i in range(3):
@@ -390,42 +430,33 @@
         value = [total[k : k + 1, :] for k in range(12)]
         return solve_small([value[0:3], value[3:6], value[6:9]], value[9:12])
 
-    def cut(slot, ref, j):
-        for i in range(sx):
-            for c in range(3):
-                v = ref[j, c, gx * sx + i][:, :sz]
+    for j in range(3):
+        apply(j)
+    inner(0, None, None)
+    for j in range(3, 6):
+        apply(j)
+    coeffs = coefficients(0)
+    one = jnp.ones((1, 1), jnp.float32)
+    b, m = krylov([one] + [None] * 6)
+    start, gain = b[0], [None] * 7
+    for j in range(3):
+        gain = plus(gain, scaled(coeffs[j], b[j]))
+        start = plus(start, scaled(-coeffs[j], m[j]))
+    b, m = krylov(start)
+    inner(1, start, m)
+    coeffs = coefficients(1)
+    left = start
+    for j in range(3):
+        gain = plus(gain, scaled(coeffs[j], b[j]))
+        left = plus(left, scaled(-coeffs[j], m[j]))
+    for slot, coords, out_ref in ((0, gain, inc_ref), (1, left, res_ref)):
+        for c in range(3):
+            for i in range(sx):
+                x = gx * sx + i
+                v = combine(coords, [basis[k, c, x, :, pl.ds(0, sz)] for k in range(7)])
                 for g in range(ngy):
                     own[slot, c, i, g] = v[g * sy : (g + 1) * sy]
-
-    for o in range(OUTER):
-        for j in range(3):
-            apply(j)
-        inner(o)
-        for j in range(3):
-            cut(j, basis, j)
-            if o == OUTER - 1:
-                cut(3 + j, image, j)
-        coeffs = coefficients(o)
-        for c in range(3):
-            for i in range(sx):
-                mine = [own[k, c, i, gy] for k in range(6 if o == OUTER - 1 else 3)]
-                gain = coeffs[0] * mine[0] + coeffs[1] * mine[1] + coeffs[2] * mine[2]
-                inc_ref[c, i] = gain if o == 0 else inc_ref[c, i] + gain
-                if o == OUTER - 1:
-                    res_ref[c, i] = mine[0] - (
-                        coeffs[0] * mine[3] + coeffs[1] * mine[4] + coeffs[2] * mine[5]
-                    )
-        if o < OUTER - 1:
-
-            def update(x):
-                for c in range(3):
-                    basis[0, c, x] = basis[0, c, x] - (
-                        coeffs[0] * image[0, c, x]
-                        + coeffs[1] * image[1, c, x]
-                        + coeffs[2] * image[2, c, x]
-                    )
-
-            loop(nx, update)
+                out_ref[c, i] = own[slot, c, i, gy]
 
     settle(blocks.at[pl.ds(0, n - 1)], send_sem.at[0])
     when(has_high, lambda: settle(from_low, send_sem.at[1]))
@@ -449,14 +480,13 @@
         (n, sx, sy, 128),
         (sx, sy, 128),
         (sx, sy, 128),
-        (3, 3, nx, ny, width),
-        (3, 3, nx, ny, width),
+        (7, 3, nx, ny, width),
         (9, nx, ny, width),
         (9, nx + 1, ny, width),
         (17, nx - 1, ny, width),
         (nx, ny, width),
         (nx, ny, width),
-        (6, 3, sx, grid[1], sy, sz),
+        (2, 3, sx, grid[1], sy, sz),
         (OUTER, grid[2], ROWS, 128),
     ]
     return pl.pallas_call(

time: 25.5 us -> 24 us (0.941)
  Pallas kernels: 22.7 us -> 21.2 us
    pallas_call x1, Pallas kernels: 22.7 us -> 21.2 us  [per_device(): pl.pallas_call(functools.partial(kernel, grid, shard), out_shape=(out, ou...]
where the time goes in v2:
time: 24 us; the launch traced here: 23.8 us
  Pallas kernels  21.2 us (88%)
  local copies, waits for them, and re-layouts  1.92 us (8%)
  between operations  0.65 us (3%)
    pallas_call x1, Pallas kernels, per_device(): pl.pallas_call(functools.partial(kernel, grid, shard), out_shape=(out, ou...  21.2 us
    unnamed x4, local copies, waits for them, and re-layouts  1.92 us

profile of v2, /device:TPU:0, one launch (start us, length us, event | category | flops | bytes accessed | tf_op | source)
XLA Modules:
  0.0 23.8 jit_solution(13612791079574276399)
XLA Ops:
  0.6 21.2 %shard_map.68 = (f32[3,2,4,128]{3,2,1,0:T(4,128)}, f32[3,2,4,128]{3,2,1,0:T(4,128)}) custom-call(f32[3,2,4,128]{3,2,1,0:T(4,128)} %disp_hbm.1, f32[3,2,4,128]{3,2,1,0:T(4,128)} %load_hbm.1, s32[2,4,128]{2,1,0:T(4,128)} %mat_hbm.1, s32[2,4,128]{2,1,0:T(4,128)} %free_hbm.1, f32[3,8]{1,0:T(4,128)} %bitcast.1), custom_call_target="tpu_custom_call" | custom-call | tf_op jit(solution)/shard_map/pallas_call | solution.py:492
  21.8 0.0 copy-start
  21.8 1.3 %copy.9 = f32[3,2,4,128]{3,2,1,0:T(4,128)} copy(f32[3,2,4,128]{3,2,1,0:T(4,128)} %get-tuple-element.4) | data formatting | bytes 24576
  23.2 0.0 copy-done
  23.2 0.6 %copy.10 = f32[3,2,4,128]{3,2,1,0:T(4,128)} copy(f32[3,2,4,128]{3,2,1,0:T(4,128)S(1)} %copy-done) | data formatting | bytes 24576
Async XLA Ops:
  21.8 1.3 %copy-start = (f32[3,2,4,128]{3,2,1,0:T(4,128)S(1)}, f32[3,2,4,128]{3,2,1,0:T(4,128)}, u32[]{:S(2)}) copy-start(f32[3,2,4,128]{3,2,1,0:T(4,128)} %get-tuple-element.5) | copy-start | bytes 36868

commit v3 on v2

--- a/solution.py
+++ b/solution.py
@@ -12,6 +12,7 @@
 HALF_WIDTH = 29.5
 CHAIN = SHIFTS + (30.5,) + SHIFTS + (30.5,)
 FIELDS = 8
+FIRST = 5
 STRIP = 16
 ROWS = 16
 MESH = pl.DeviceIdType.MESH
@@ -99,7 +100,7 @@
 
     fetched = [
         fetch(disp_hbm, blocks.at[me, pl.ds(0, 3)], 0),
-        fetch(load_hbm, blocks.at[me, pl.ds(3, 3)], 1),
+        fetch(load_hbm, blocks.at[me, pl.ds(FIRST, 3)], 1),
         fetch(mat_hbm, flags.at[0], 2),
         fetch(free_hbm, flags.at[1], 3),
         fetch(table_hbm, table_ref, 4),
@@ -115,16 +116,16 @@
     def peers(count, first, body):
         loop(count, lambda k: body(lax.rem(me + first + k, n)))
 
-    peers(n - 1, 1, lambda p: greet(p, gz))
     when(has_low, lambda: peers(n, 0, lambda p: greet(p, gz - 1)))
     when(has_high, lambda: peers(n, 0, lambda p: greet(p, gz + 1)))
     for z in range(ngz):
         when((z > gz + 1) | (z < gz - 1), lambda z=z: greet(me, z))
+    peers(n - 1, 1, lambda p: greet(p, gz))
 
     for copy in fetched[:4]:
         copy.wait()
-    blocks[me, 6] = flags[0].astype(jnp.float32)
-    blocks[me, 7] = flags[1].astype(jnp.float32)
+    blocks[me, 3] = flags[0].astype(jnp.float32)
+    blocks[me, 4] = flags[1].astype(jnp.float32)
     lane = lax.broadcasted_iota(jnp.int32, (sy, 128), 1)
     for i in range(sx):
         low = jnp.zeros((sy, 128), jnp.float32)
@@ -163,7 +164,6 @@
             device_id_type=MESH,
         ).start()
 
-    peers(n - 1, 1, lambda p: send(blocks.at[me], blocks.at[me], 0, p, gz))
     when(
         has_high,
         lambda: peers(n, 0, lambda p: send(to_high, from_low.at[me], 1, p, gz + 1)),
@@ -173,6 +173,13 @@
         lambda: peers(n, 0, lambda p: send(to_low, from_high.at[me], 2, p, gz - 1)),
     )
 
+    early = blocks.at[me, pl.ds(0, FIRST)]
+    late = blocks.at[me, pl.ds(FIRST, FIELDS - FIRST)]
+    peers(n - 1, 1, lambda p: send(early, early, 0, p, gz))
+    peers(n - 1, 1, lambda p: send(late, late, 3, p, gz))
+    early_all = blocks.at[pl.ds(0, n - 1), pl.ds(0, FIRST)]
+    late_all = blocks.at[pl.ds(0, n - 1), pl.ds(FIRST, FIELDS - FIRST)]
+
     def settle(ref, sem):
         pltpu.make_async_copy(ref, ref, sem).wait()
 
@@ -180,7 +187,7 @@
         piola[e, 0] = jnp.zeros((ny, width), jnp.float32)
         piola[e, nx] = jnp.zeros((ny, width), jnp.float32)
 
-    settle(blocks.at[pl.ds(0, n - 1)], recv_sem.at[0])
+    settle(early_all, recv_sem.at[0])
     when(has_low, lambda: settle(from_low, recv_sem.at[1]))
     when(has_high, lambda: settle(from_high, recv_sem.at[2]))
 
@@ -198,12 +205,10 @@
 
     def unpack(x):
         after, before = rows(from_high, (), x), rows(from_low, (), x)
-        free = whole_rows(7, x, after, before)
-        freeb[x] = free
+        freeb[x] = whole_rows(4, x, after, before)
         for c in range(3):
             basis[1, c, x] = whole_rows(c, x, after, before)
-            basis[0, c, x] = whole_rows(3 + c, x, after, before) * free
-        basis[2, 0, x] = whole_rows(6, x, after, before)
+        basis[2, 0, x] = whole_rows(3, x, after, before)
 
     loop(nx, unpack)
 
@@ -430,6 +435,15 @@
         value = [total[k : k + 1, :] for k in range(12)]
         return solve_small([value[0:3], value[3:6], value[6:9]], value[9:12])
 
+    settle(late_all, recv_sem.at[3])
+
+    def begin(x):
+        after, before = rows(from_high, (), x), rows(from_low, (), x)
+        for c in range(3):
+            basis[0, c, x] = freeb[x] * whole_rows(FIRST + c, x, after, before)
+
+    loop(nx, begin)
+
     for j in range(3):
         apply(j)
     inner(0, None, None)
@@ -458,7 +472,8 @@
                     own[slot, c, i, g] = v[g * sy : (g + 1) * sy]
                 out_ref[c, i] = own[slot, c, i, gy]
 
-    settle(blocks.at[pl.ds(0, n - 1)], send_sem.at[0])
+    settle(early_all, send_sem.at[0])
+    settle(late_all, send_sem.at[3])
     when(has_high, lambda: settle(from_low, send_sem.at[1]))
     when(has_low, lambda: settle(from_high, send_sem.at[2]))
     for o in range(OUTER):
@@ -499,8 +514,8 @@
             pltpu.VMEM((2, sx, sy, sz), jnp.int32),
             pltpu.SMEM(table.shape[::-1], f32),
             pltpu.SemaphoreType.DMA((5,)),
-            pltpu.SemaphoreType.DMA((3,)),
-            pltpu.SemaphoreType.DMA((3,)),
+            pltpu.SemaphoreType.DMA((4,)),
+            pltpu.SemaphoreType.DMA((4,)),
             pltpu.SemaphoreType.DMA((OUTER,)),
             pltpu.SemaphoreType.DMA((OUTER,)),
         ],

time: 24 us -> 24.3 us (1.012)
  Pallas kernels: 21.2 us -> 21.5 us
    pallas_call x1, Pallas kernels: 21.2 us -> 21.5 us  [per_device(): pl.pallas_call(functools.partial(kernel, grid, shard), out_shape=(out, ou...]
where the time goes in v3:
time: 24.3 us; the launch traced here: 24.1 us
  Pallas kernels  21.5 us (88%)
  local copies, waits for them, and re-layouts  1.92 us (8%)
  between operations  0.65 us (3%)
    pallas_call x1, Pallas kernels, per_device(): pl.pallas_call(functools.partial(kernel, grid, shard), out_shape=(out, ou...  21.5 us
    unnamed x4, local copies, waits for them, and re-layouts  1.92 us

profile of v3, /device:TPU:0, one launch (start us, length us, event | category | flops | bytes accessed | tf_op | source)
XLA Modules:
  0.0 24.1 jit_solution(5317168659416779124)
XLA Ops:
  0.6 21.5 %shard_map.68 = (f32[3,2,4,128]{3,2,1,0:T(4,128)}, f32[3,2,4,128]{3,2,1,0:T(4,128)}) custom-call(f32[3,2,4,128]{3,2,1,0:T(4,128)} %disp_hbm.1, f32[3,2,4,128]{3,2,1,0:T(4,128)} %load_hbm.1, s32[2,4,128]{2,1,0:T(4,128)} %mat_hbm.1, s32[2,4,128]{2,1,0:T(4,128)} %free_hbm.1, f32[3,8]{1,0:T(4,128)} %bitcast.1), custom_call_target="tpu_custom_call" | custom-call | tf_op jit(solution)/shard_map/pallas_call | solution.py:507
  22.2 0.0 copy-start
  22.2 1.3 %copy.9 = f32[3,2,4,128]{3,2,1,0:T(4,128)} copy(f32[3,2,4,128]{3,2,1,0:T(4,128)} %get-tuple-element.4) | data formatting | bytes 24576
  23.5 0.0 copy-done
  23.5 0.6 %copy.10 = f32[3,2,4,128]{3,2,1,0:T(4,128)} copy(f32[3,2,4,128]{3,2,1,0:T(4,128)S(1)} %copy-done) | data formatting | bytes 24576
Async XLA Ops:
  22.2 1.3 %copy-start = (f32[3,2,4,128]{3,2,1,0:T(4,128)S(1)}, f32[3,2,4,128]{3,2,1,0:T(4,128)}, u32[]{:S(2)}) copy-start(f32[3,2,4,128]{3,2,1,0:T(4,128)} %get-tuple-element.5) | copy-start | bytes 36868
